TPU v7x, 32 devices: a whole 2x2x4 slice. The times are simulated.
32 devices in a mesh: comp: 16 (over z, y, core), io: 2 (over x).
Axes of the slice: x: 2, y: 2, z: 4, core: 2. Of those that a mesh axis runs over, the one named last changes fastest.
Arguments:
- tracer: float32 [40, 32, 2048], P(None, 'io', 'comp'), may hold values from -6 to 6
- anchor: float32 [40, 32, 2048], P(None, 'io', 'comp'), may hold values from -6 to 6
- east_flow: float32 [40, 32, 2048], P(None, 'io', 'comp'), may hold values from -0.15 to 0.15
- north_flow: float32 [40, 32, 2048], P(None, 'io', 'comp'), may hold values from -0.15 to 0.15
- diffusivity: float32 [40, 32, 2048], P(None, 'io', 'comp'), may hold values from 0.01 to 0.08
- land_mask: int32 [32, 2048], P('io', 'comp'), may hold values from 0 to 1, as said below
- block_dest: int32 [16, 32, 1], P('comp', 'io'), may hold values from 0 to 1; in each aligned block of 16 rows (0 to 15, 16 to 31, ..., all dimensions but the last counted through in order) at most 12 rows name the same one
Outputs:
- tracer_out: float32 [40, 32, 2048], P(None, 'io', 'comp')
- restart: float32 [4, 12, 40, 2048], P('io', None, None, 'comp')
- partner_copy: float32 [4, 12, 40, 2048], P('io', None, None, 'comp')
Inputs may be any that keep to these rules, and one draw needn't show every extreme that they name: `land_mask`: the first and the last of the 32 rows are land. `block_dest`: among the 16 blocks of one tile no aggregator is named more than 12 times.
All inputs are finite; a program needn't handle non-finite values.
Results may differ from a plain program's by a relative error of at most 0.0003.
Values sent between devices are 32-bit elements; how exact they have to be, the bound alone decides.
A program may use at most 64 MiB of HBM per device.

v0:
```python
import jax
import jax.numpy as jnp
from jax import lax
from jax.sharding import PartitionSpec as P

BLK = 128


def with_halo(block, sides, width):
    for axis, dim in sides:
        count = lax.axis_size(axis)
        forward = [(i, i + 1) for i in range(count - 1)]
        forward.append((count - 1, 0))
        backward = [(target, source) for source, target in forward]
        low = lax.ppermute(
            lax.slice_in_dim(block, block.shape[dim] - width, None, axis=dim), axis, forward
        )
        high = lax.ppermute(lax.slice_in_dim(block, 0, width, axis=dim), axis, backward)
        block = jnp.concatenate([low, block, high], axis=dim)
    return block


def from_behind(array, axis, by):
    devices = lax.axis_size(axis)
    return lax.ppermute(array, axis, [(i, (i + by) % devices) for i in range(devices)])


def advance(padded, east_pad, north_pad, diff_pad, ocean_pad):
    east_open = ocean_pad[:, :-1] * ocean_pad[:, 1:]
    north_open = ocean_pad[:-1, :] * ocean_pad[1:, :]
    here_e = padded[:, :, :-1]
    field_e = padded[:, :, 1:]
    flow_e = east_pad[:, :, :-1]
    flux_east = east_open * (
        jnp.maximum(flow_e, 0.0) * here_e
        + jnp.minimum(flow_e, 0.0) * field_e
        - diff_pad[:, :, :-1] * (field_e - here_e)
    )
    here_n = padded[:, :-1, :]
    field_n = padded[:, 1:, :]
    flow_n = north_pad[:, :-1, :]
    flux_north = north_open * (
        jnp.maximum(flow_n, 0.0) * here_n
        + jnp.minimum(flow_n, 0.0) * field_n
        - diff_pad[:, :-1, :] * (field_n - here_n)
    )
    centre = padded[:, 1:-1, 1:-1]
    return (
        centre
        - (flux_east[:, 1:-1, 1:] - flux_east[:, 1:-1, :-1])
        - (flux_north[:, 1:, 1:-1] - flux_north[:, :-1, 1:-1])
    )


def pack_blocks(delta, land_mask, block_dest, n_aggr, block_cols):
    levels = delta.shape[0]
    total = land_mask.shape[0] * land_mask.shape[1]
    nblocks = total // block_cols
    capacity = max(2, 3 * nblocks // (2 * n_aggr))
    flat_mask = land_mask.reshape(total)
    places = jnp.cumsum(flat_mask, dtype=jnp.int32) - 1
    target = jnp.where(flat_mask == 1, places, total)
    packed = (
        jnp.zeros((levels, total + 1), jnp.float32)
        .at[:, target]
        .set(delta.reshape(levels, total))[:, :total]
    )
    blocks = packed.reshape(levels, nblocks, block_cols)
    dest = block_dest.reshape(nblocks)
    onehot = (dest[:, None] == jnp.arange(n_aggr, dtype=jnp.int32)[None, :]).astype(jnp.int32)
    earlier = jnp.cumsum(onehot, axis=0, dtype=jnp.int32) - onehot
    ranks = jnp.sum(earlier * onehot, axis=1, dtype=jnp.int32)
    slots = dest * capacity + ranks
    select = (jnp.arange(n_aggr * capacity, dtype=jnp.int32)[:, None] == slots[None, :]).astype(
        jnp.float32
    )
    sendbuf = jnp.einsum("qk,lkb->qlb", select, blocks, precision=lax.Precision.HIGHEST)
    return sendbuf.reshape(n_aggr, capacity, levels, block_cols)


def per_device(tracer, anchor, east_flow, north_flow, diffusivity, land_mask, block_dest):
    levels = tracer.shape[0]
    static = jnp.concatenate(
        [east_flow, north_flow, diffusivity, land_mask.astype(jnp.float32)[None]], axis=0
    )
    static_pad = with_halo(static, (("comp", 2), ("io", 1)), 1)
    east_pad = static_pad[0:levels]
    north_pad = static_pad[levels : 2 * levels]
    diff_pad = static_pad[2 * levels : 3 * levels]
    ocean_pad = static_pad[3 * levels]
    field = tracer
    for step in range(2):
        padded = with_halo(field, (("comp", 2), ("io", 1)), 1)
        field = advance(padded, east_pad, north_pad, diff_pad, ocean_pad)
    delta = field - anchor
    n_aggr = lax.axis_size("io")
    half_loop = lax.axis_size("comp") // 2
    sendbuf = pack_blocks(delta, land_mask, block_dest, n_aggr, BLK)
    restart = lax.all_to_all(sendbuf, "io", split_axis=0, concat_axis=0, tiled=True)
    partner_copy = from_behind(restart, "comp", half_loop)
    return (field, restart, partner_copy)


def solution(mesh):
    placed = (
        P(None, "io", "comp"),
        P(None, "io", "comp"),
        P(None, "io", "comp"),
        P(None, "io", "comp"),
        P(None, "io", "comp"),
        P("io", "comp"),
        P("comp", "io", None),
    )
    return jax.shard_map(
        per_device,
        mesh=mesh,
        in_specs=placed,
        out_specs=(P(None, "io", "comp"), P("io", None, None, "comp"), P("io", None, None, "comp")),
        check_vma=False,
    )
```

profile of v0, /device:TPU:0, one launch (start us, length us, event | category | flops | bytes accessed | tf_op | source)
XLA Modules:
  0.0 98.3 jit_solution(16448509542483686791)
XLA Ops:
  0.6 2.0 %fusion.19 = (f32[40,16,1]{2,1,0:T(8,128)}, f32[40,16,1]{2,1,0:T(8,128)}) fusion(f32[40,16,128]{2,1,0:T(8,128)} %param.7), kind=kLoop, calls=%fused_computation.72 | loop fusion | bytes 10240 | tf_op jit(solution)/shard_map/slice | solution.py:16
  2.6 5.4 %collective-permute-start.5 = (f32[40,16,1]{2,1,0:T(8,128)}, f32[40,16,1]{2,1,0:T(8,128)}, u32[]{:S(2)}, u32[]{:S(2)}) collective-permute-start(f32[40,16,1]{2,1,0:T(8,128)} %get-tuple-element.31), channel_id=1, source_target_pairs={{2,0},{4,2},{6,4},{8,6},{10,8},{12,10},{14,12},{16,14},{18,16},{20... | collective-permute-start | bytes 7688 | tf_op jit(solution)/shard_map/ppermute | solution.py:18
  8.1 1.0 reduce-window.9
  9.3 0.8 add_select_fusion
  10.1 1.2 %pad_maximum_fusion.1 = f32[121,16,128]{2,1,0:T(8,128)S(1)} fusion(f32[1,16,128]{2,1,0:T(8,128)S(1)} %get-tuple-element.33, f32[40,16,128]{2,1,0:T(8,128)} %param.11, f32[40,16,128]{2,1,0:T(8,128)} %param.10, f32[40,16,128]{2,1,0:T(8,128)} %param.9), kind=kLoop, calls=%fused_computation.2 | loop fusion | flops 743424 | bytes 1982464 | tf_op jit(solution)/shard_map/concatenate | solution.py:83
  11.8 0.4 copy.56
  12.2 4.5 %collective-permute-start.1 = (f32[121,16,1]{0,1,2:T(8,128)S(1)}, f32[121,16,1]{0,1,2:T(8,128)S(1)}, u32[]{:S(2)}, u32[]{:S(2)}) collective-permute-start(f32[121,16,1]{0,1,2:T(8,128)S(1)} %copy.56), channel_id=1, source_target_pairs={{2,0},{4,2},{6,4},{8,6},{10,8},{12,10},{14,12},{16,14},{18,16},{20... | collective-permute-start | bytes 23240 | tf_op jit(solution)/shard_map/ppermute | solution.py:18
  16.6 0.4 copy.55
  17.1 0.6 compare_select_fusion
  17.8 0.8 select_reduce_fusion
  18.6 2.1 %pad_maximum_fusion.24 = (f32[40,1,130]{2,1,0:T(1,128)}, f32[40,1,130]{2,1,0:T(1,128)}) fusion(f32[40,16,1]{2,1,0:T(8,128)} %collective-permute-done.5, f32[40,16,128]{2,1,0:T(8,128)S(1)} %copy-done, f32[40,16,1]{2,1,0:T(8,128)} %collective-permute-done.4), kind=kLoop, calls=%fused_computation.46 | loop fusion | flops 20800 | bytes 374400 | tf_op jit(solution)/shard_map/slice | solution.py:16
  20.7 1.5 %collective-permute-start.7 = (f32[40,1,130]{2,1,0:T(1,128)}, f32[40,1,130]{2,1,0:T(1,128)}, u32[]{:S(2)}, u32[]{:S(2)}) collective-permute-start(f32[40,1,130]{2,1,0:T(1,128)} %get-tuple-element.27), channel_id=1, source_target_pairs={{1,0},{0,1},{3,2},{2,3},{5,4},{4,5},{7,6},{6,7},{9,8},{8,9},{11,10... | collective-permute-start | bytes 62408 | tf_op jit(solution)/shard_map/ppermute | solution.py:18
  22.2 0.5 collective-permute-start.6
  22.7 0.5 copy.58
  23.3 0.5 copy.57
  23.8 0.8 pad_maximum_fusion.18
  24.7 0.7 copy.60
  25.4 1.5 %collective-permute-start.3 = (f32[121,1,130]{0,2,1:T(8,128)}, f32[121,1,130]{0,2,1:T(8,128)}, u32[]{:S(2)}, u32[]{:S(2)}) collective-permute-start(f32[121,1,130]{0,2,1:T(8,128)} %copy.60), channel_id=1, source_target_pairs={{1,0},{0,1},{3,2},{2,3},{5,4},{4,5},{7,6},{6,7},{9,8},{8,9},{11,10... | collective-permute-start | bytes 188768 | tf_op jit(solution)/shard_map/ppermute | solution.py:18
  26.9 0.7 copy.59
  27.7 0.5 collective-permute-start.2
  28.2 1.6 %pad_maximum_fusion.9 = f32[40,18,130]{2,1,0:T(8,128)S(1)} fusion(f32[40,1,130]{2,1,0:T(1,128)} %collective-permute-done.7, f32[40,16,1]{2,1,0:T(8,128)} %collective-permute-done.5, f32[40,16,128]{2,1,0:T(8,128)S(1)} %copy-done, f32[40,16,1]{2,1,0:T(8,128)} %collective-permute-done.4, f32[40,1,130]{2,1,0:T(1,128)} %collective-permute-done.6), kind=kLoop, calls=%fused_computation.10 | loop fusion | flops 374400 | bytes 748800 | tf_op jit(solution)/shard_map/concatenate | solution.py:19
  30.0 1.0 %copy.62 = f32[121,1,130]{2,1,0:T(1,128)S(1)} copy(f32[121,1,130]{0,2,1:T(8,128)} %collective-permute-done.3) | data formatting | bytes 125840 | tf_op jit(solution)/shard_map/ppermute | solution.py:18
  31.1 1.2 %collective-permute-done.2 = f32[121,1,130]{0,2,1:T(8,128)} collective-permute-done((f32[121,1,130]{0,2,1:T(8,128)}, f32[121,1,130]{0,2,1:T(8,128)}, u32[]{:S(2)}, u32[]{:S(2)}) %collective-permute-start.2) | collective-permute-done | bytes 62952 | tf_op jit(solution)/shard_map/ppermute | solution.py:15
  32.3 1.0 %copy.61 = f32[121,1,130]{2,1,0:T(1,128)S(1)} copy(f32[121,1,130]{0,2,1:T(8,128)} %collective-permute-done.2) | data formatting | bytes 125840 | tf_op jit(solution)/shard_map/ppermute | solution.py:15
  33.4 0.8 copy-done.2
  34.5 1.4 %pad_maximum_fusion = f32[121,18,130]{2,1,0:T(8,128)S(1)} fusion(f32[121,1,130]{2,1,0:T(1,128)S(1)} %copy.62, f32[121,16,1]{2,1,0:T(8,128)S(1)} %copy.58, f32[1,16,128]{2,1,0:T(8,128)S(1)} %get-tuple-element.33, f32[40,16,128]{2,1,0:T(8,128)S(1)} %copy-done.2, f32[40,16,128]{2,1,0:T(8,128)S(1)} %copy-done.4, f32[40,16,128]{2,1,0:T(8,128)S(1)} %copy-done.6, ...), kind=kLoop, calls=%fused_computation.1 | loop fusion | flops 1981980 | bytes 2265120 | tf_op jit(solution)/shard_map/concatenate | solution.py:19
  35.9 0.4 subtract_multiply_fusion.3
  36.3 5.3 %subtract_multiply_fusion.2 = (f32[40,17,130]{2,1,0:T(8,128)S(1)}, f32[40,17,130]{2,1,0:T(8,128)S(1)}, f32[40,17,130]{2,1,0:T(8,128)S(1)}) fusion(f32[40,1,130]{2,1,0:T(1,128)} %collective-permute-done.7, f32[40,16,1]{2,1,0:T(8,128)} %collective-permute-done.5, f32[40,16,128]{2,1,0:T(8,128)S(1)} %copy-done, f32[40,16,1]{2,1,0:T(8,128)} %collective-permute-done.4, ...), kind=kLoop, calls=%fused_computation.18 | loop fusion | flops 2386800 | bytes 2513680 | tf_op jit(solution)/shard_map/mul | solution.py:42
  41.6 0.3 fusion.4
  42.1 2.5 %collective-permute-start.9 = (f32[40,16,1]{2,1,0:T(8,128)S(1)}, f32[40,16,1]{2,1,0:T(8,128)S(1)}, u32[]{:S(2)}, u32[]{:S(2)}) collective-permute-start(f32[40,16,1]{2,1,0:T(8,128)S(1)} %get-tuple-element.29), channel_id=1, source_target_pairs={{2,0},{4,2},{6,4},{8,6},{10,8},{12,10},{14,12},{16,14},{18,16},{20... | collective-permute-start | bytes 7688 | tf_op jit(solution)/shard_map/ppermute | solution.py:18
  44.7 4.6 %collective-permute-done.9 = f32[40,16,1]{2,1,0:T(8,128)S(1)} collective-permute-done((f32[40,16,1]{2,1,0:T(8,128)S(1)}, f32[40,16,1]{2,1,0:T(8,128)S(1)}, u32[]{:S(2)}, u32[]{:S(2)}) %collective-permute-start.9) | collective-permute-done | bytes 2592 | tf_op jit(solution)/shard_map/ppermute | solution.py:18
  49.2 4.6 %collective-permute-done.8 = f32[40,16,1]{2,1,0:T(8,128)S(1)} collective-permute-done((f32[40,16,1]{2,1,0:T(8,128)S(1)}, f32[40,16,1]{2,1,0:T(8,128)S(1)}, u32[]{:S(2)}, u32[]{:S(2)}) %collective-permute-start.8) | collective-permute-done | bytes 2592 | tf_op jit(solution)/shard_map/ppermute | solution.py:15
  54.2 0.9 collective-permute-start.11
  55.1 1.2 %collective-permute-start.10 = (f32[40,1,130]{2,1,0:T(1,128)S(1)}, f32[40,1,130]{2,1,0:T(1,128)S(1)}, u32[]{:S(2)}, u32[]{:S(2)}) collective-permute-start(f32[40,1,130]{2,1,0:T(1,128)S(1)} %get-tuple-element.24), channel_id=1, source_target_pairs={{0,1},{1,0},{2,3},{3,2},{4,5},{5,4},{6,7},{7,6},{8,9},{9,8},{10,11... | collective-permute-start | bytes 62408 | tf_op jit(solution)/shard_map/ppermute | solution.py:15
  56.2 2.0 %collective-permute-done.11 = f32[40,1,130]{2,1,0:T(1,128)S(1)} collective-permute-done((f32[40,1,130]{2,1,0:T(1,128)S(1)}, f32[40,1,130]{2,1,0:T(1,128)S(1)}, u32[]{:S(2)}, u32[]{:S(2)}) %collective-permute-start.11) | collective-permute-done | bytes 20832 | tf_op jit(solution)/shard_map/ppermute | solution.py:18
  58.2 0.9 collective-permute-done.10
  59.1 0.5 pad_maximum_fusion.11
  59.5 0.5 subtract_multiply_fusion.1
  60.1 0.9 subtract_multiply_fusion
  61.0 1.0 %fusion.15 = (f32[40,16,128]{2,1,0:T(8,128)S(1)}, f32[40,16,128]{2,1,0:T(8,128)}) fusion(f32[40,16,128]{2,1,0:T(8,128)S(1)} %copy-done.7, f32[40,17,130]{2,1,0:T(8,128)S(1)} %subtract_multiply_fusion, f32[40,16,128]{2,1,0:T(8,128)S(1)} %fusion.4, f32[40,18,129]{2,1,0:T(8,128)S(1)} %subtract_multiply_fusion.1), kind=kLoop, calls=%fused_computation.69 | loop fusion | flops 409600 | bytes 2621440 | tf_op jit(solution)/shard_map/sub | solution.py:95
  62.1 0.3 copy.69
  62.4 6.0 %scatter_custom_fusion = f32[40,2049]{0,1:T(8,128)S(1)} fusion(s32[2048]{0:T(1024)} %bitcast.25, f32[2048,40]{1,0:T(8,128)S(1)} %bitcast.23, f32[]{:T(128)} %constant.7.clone.1), kind=kCustom, calls=%fused_computation.22 | custom fusion | bytes 328352 | tf_op jit(solution)/shard_map/scatter | solution.py:66
  68.5 0.3 copy.70
  68.8 0.5 fusion.6
  69.5 8.8 %all_to_all.5 = f32[2,12,40,128]{3,2,1,0:T(8,128)S(1)} all-to-all(f32[2,12,40,128]{3,2,1,0:T(8,128)S(1)} %copy.67), channel_id=1, replica_groups=mesh['comp'=16,'io'=2] {'io'}, dimensions={0} | all-to-all | bytes 983040 | tf_op jit(solution)/shard_map/all_to_all | solution.py:99
  78.3 18.5 %collective-permute-done.12 = f32[2,12,40,128]{3,2,1,0:T(8,128)S(1)} collective-permute-done((f32[2,12,40,128]{3,2,1,0:T(8,128)S(1)}, f32[2,12,40,128]{3,2,1,0:T(8,128)S(1)}, u32[]{:S(2)}, u32[]{:S(2)}) %collective-permute-start.12) | collective-permute-done | bytes 491552 | tf_op jit(solution)/shard_map/ppermute | solution.py:25
  96.8 0.8 copy.73
  97.6 0.8 copy.74
  (47 shorter events, 2.2 us)
Async XLA Ops:
  2.6 16.0 %collective-permute-start.5 = (f32[40,16,1]{2,1,0:T(8,128)}, f32[40,16,1]{2,1,0:T(8,128)}, u32[]{:S(2)}, u32[]{:S(2)}) collective-permute-start(f32[40,16,1]{2,1,0:T(8,128)} %get-tuple-element.31), channel_id=1, source_target_pairs={{2,0},{4,2},{6,4},{8,6},{10,8},{12,10},{14,12},{16,14},{18,16},{20... | collective-permute-start | bytes 7688 | tf_op jit(solution)/shard_map/ppermute | solution.py:18
  8.1 10.5 %collective-permute-start.4 = (f32[40,16,1]{2,1,0:T(8,128)}, f32[40,16,1]{2,1,0:T(8,128)}, u32[]{:S(2)}, u32[]{:S(2)}) collective-permute-start(f32[40,16,1]{2,1,0:T(8,128)} %get-tuple-element.30), channel_id=1, source_target_pairs={{0,2},{2,4},{4,6},{6,8},{8,10},{10,12},{12,14},{14,16},{16,18},{18... | collective-permute-start | bytes 7688 | tf_op jit(solution)/shard_map/ppermute | solution.py:15
  11.4 6.3 %copy-start.8 = (s32[1,16,1]{1,2,0:T(1,128)S(1)}, s32[1,16,1]{1,2,0:T(1,128)}, u32[]{:S(2)}) copy-start(s32[1,16,1]{1,2,0:T(1,128)} %param.13) | copy-start | bytes 196
  11.4 7.2 %copy-start = (f32[40,16,128]{2,1,0:T(8,128)S(1)}, f32[40,16,128]{2,1,0:T(8,128)}, u32[]{:S(2)}) copy-start(f32[40,16,128]{2,1,0:T(8,128)} %param.7) | copy-start | bytes 983044
  11.7 12.1 %copy-start.1 = (f32[40,16,128]{2,1,0:T(8,128)S(1)}, f32[40,16,128]{2,1,0:T(8,128)}, u32[]{:S(2)}) copy-start(f32[40,16,128]{2,1,0:T(8,128)} %param.11) | copy-start | bytes 983044
  11.7 12.1 %copy-start.3 = (f32[40,16,128]{2,1,0:T(8,128)S(1)}, f32[40,16,128]{2,1,0:T(8,128)}, u32[]{:S(2)}) copy-start(f32[40,16,128]{2,1,0:T(8,128)} %param.10) | copy-start | bytes 983044
  11.7 12.1 %copy-start.5 = (f32[40,16,128]{2,1,0:T(8,128)S(1)}, f32[40,16,128]{2,1,0:T(8,128)}, u32[]{:S(2)}) copy-start(f32[40,16,128]{2,1,0:T(8,128)} %param.9) | copy-start | bytes 983044
  12.2 10.5 %collective-permute-start.1 = (f32[121,16,1]{0,1,2:T(8,128)S(1)}, f32[121,16,1]{0,1,2:T(8,128)S(1)}, u32[]{:S(2)}, u32[]{:S(2)}) collective-permute-start(f32[121,16,1]{0,1,2:T(8,128)S(1)} %copy.56), channel_id=1, source_target_pairs={{2,0},{4,2},{6,4},{8,6},{10,8},{12,10},{14,12},{16,14},{18,16},{20... | collective-permute-start | bytes 23240 | tf_op jit(solution)/shard_map/ppermute | solution.py:18
  17.1 6.2 %collective-permute-start = (f32[121,16,1]{0,1,2:T(8,128)S(1)}, f32[121,16,1]{0,1,2:T(8,128)S(1)}, u32[]{:S(2)}, u32[]{:S(2)}) collective-permute-start(f32[121,16,1]{0,1,2:T(8,128)S(1)} %copy.55), channel_id=1, source_target_pairs={{0,2},{2,4},{4,6},{6,8},{8,10},{10,12},{12,14},{14,16},{16,18},{18... | collective-permute-start | bytes 23240 | tf_op jit(solution)/shard_map/ppermute | solution.py:15
  20.7 7.5 %collective-permute-start.7 = (f32[40,1,130]{2,1,0:T(1,128)}, f32[40,1,130]{2,1,0:T(1,128)}, u32[]{:S(2)}, u32[]{:S(2)}) collective-permute-start(f32[40,1,130]{2,1,0:T(1,128)} %get-tuple-element.27), channel_id=1, source_target_pairs={{1,0},{0,1},{3,2},{2,3},{5,4},{4,5},{7,6},{6,7},{9,8},{8,9},{11,10... | collective-permute-start | bytes 62408 | tf_op jit(solution)/shard_map/ppermute | solution.py:18
  22.2 6.0 %collective-permute-start.6 = (f32[40,1,130]{2,1,0:T(1,128)}, f32[40,1,130]{2,1,0:T(1,128)}, u32[]{:S(2)}, u32[]{:S(2)}) collective-permute-start(f32[40,1,130]{2,1,0:T(1,128)} %get-tuple-element.26), channel_id=1, source_target_pairs={{0,1},{1,0},{2,3},{3,2},{4,5},{5,4},{6,7},{7,6},{8,9},{9,8},{10,11... | collective-permute-start | bytes 62408 | tf_op jit(solution)/shard_map/ppermute | solution.py:15
  25.4 4.6 %collective-permute-start.3 = (f32[121,1,130]{0,2,1:T(8,128)}, f32[121,1,130]{0,2,1:T(8,128)}, u32[]{:S(2)}, u32[]{:S(2)}) collective-permute-start(f32[121,1,130]{0,2,1:T(8,128)} %copy.60), channel_id=1, source_target_pairs={{1,0},{0,1},{3,2},{2,3},{5,4},{4,5},{7,6},{6,7},{9,8},{8,9},{11,10... | collective-permute-start | bytes 188768 | tf_op jit(solution)/shard_map/ppermute | solution.py:18
  27.7 4.6 %collective-permute-start.2 = (f32[121,1,130]{0,2,1:T(8,128)}, f32[121,1,130]{0,2,1:T(8,128)}, u32[]{:S(2)}, u32[]{:S(2)}) collective-permute-start(f32[121,1,130]{0,2,1:T(8,128)} %copy.59), channel_id=1, source_target_pairs={{0,1},{1,0},{2,3},{3,2},{4,5},{5,4},{6,7},{7,6},{8,9},{9,8},{10,11... | collective-permute-start | bytes 188768 | tf_op jit(solution)/shard_map/ppermute | solution.py:15
  33.3 1.0 copy-start.2
  33.3 1.1 %copy-start.4 = (f32[40,16,128]{2,1,0:T(8,128)S(1)}, f32[40,16,128]{2,1,0:T(8,128)}, u32[]{:S(2)}) copy-start(f32[40,16,128]{2,1,0:T(8,128)} %param.10) | copy-start | bytes 983044
  33.3 1.2 %copy-start.6 = (f32[40,16,128]{2,1,0:T(8,128)S(1)}, f32[40,16,128]{2,1,0:T(8,128)}, u32[]{:S(2)}) copy-start(f32[40,16,128]{2,1,0:T(8,128)} %param.9) | copy-start | bytes 983044
  41.6 3.0 %copy-start.9 = (s32[1,16,1]{1,2,0:T(1,128)S(1)}, s32[1,16,1]{1,2,0:T(1,128)}, u32[]{:S(2)}) copy-start(s32[1,16,1]{1,2,0:T(1,128)} %param.13) | copy-start | bytes 196
  41.6 3.0 %copy-start.10 = (s32[16]{0:T(128)S(1)}, s32[16]{0:T(128)}, u32[]{:S(2)}) copy-start(s32[16]{0:T(128)} %select_reduce_fusion) | copy-start | bytes 196
  42.1 7.1 %collective-permute-start.9 = (f32[40,16,1]{2,1,0:T(8,128)S(1)}, f32[40,16,1]{2,1,0:T(8,128)S(1)}, u32[]{:S(2)}, u32[]{:S(2)}) collective-permute-start(f32[40,16,1]{2,1,0:T(8,128)S(1)} %get-tuple-element.29), channel_id=1, source_target_pairs={{2,0},{4,2},{6,4},{8,6},{10,8},{12,10},{14,12},{16,14},{18,16},{20... | collective-permute-start | bytes 7688 | tf_op jit(solution)/shard_map/ppermute | solution.py:18
  44.6 9.2 %collective-permute-start.8 = (f32[40,16,1]{2,1,0:T(8,128)S(1)}, f32[40,16,1]{2,1,0:T(8,128)S(1)}, u32[]{:S(2)}, u32[]{:S(2)}) collective-permute-start(f32[40,16,1]{2,1,0:T(8,128)S(1)} %get-tuple-element.28), channel_id=1, source_target_pairs={{0,2},{2,4},{4,6},{6,8},{8,10},{10,12},{12,14},{14,16},{16,18},{18... | collective-permute-start | bytes 7688 | tf_op jit(solution)/shard_map/ppermute | solution.py:15
  54.2 4.1 %collective-permute-start.11 = (f32[40,1,130]{2,1,0:T(1,128)S(1)}, f32[40,1,130]{2,1,0:T(1,128)S(1)}, u32[]{:S(2)}, u32[]{:S(2)}) collective-permute-start(f32[40,1,130]{2,1,0:T(1,128)S(1)} %get-tuple-element.25), channel_id=1, source_target_pairs={{1,0},{0,1},{3,2},{2,3},{5,4},{4,5},{7,6},{6,7},{9,8},{8,9},{11,10... | collective-permute-start | bytes 62408 | tf_op jit(solution)/shard_map/ppermute | solution.py:18
  55.1 4.0 %collective-permute-start.10 = (f32[40,1,130]{2,1,0:T(1,128)S(1)}, f32[40,1,130]{2,1,0:T(1,128)S(1)}, u32[]{:S(2)}, u32[]{:S(2)}) collective-permute-start(f32[40,1,130]{2,1,0:T(1,128)S(1)} %get-tuple-element.24), channel_id=1, source_target_pairs={{0,1},{1,0},{2,3},{3,2},{4,5},{5,4},{6,7},{7,6},{8,9},{9,8},{10,11... | collective-permute-start | bytes 62408 | tf_op jit(solution)/shard_map/ppermute | solution.py:15
  60.1 1.0 copy-start.7
  78.3 18.5 %collective-permute-start.12 = (f32[2,12,40,128]{3,2,1,0:T(8,128)S(1)}, f32[2,12,40,128]{3,2,1,0:T(8,128)S(1)}, u32[]{:S(2)}, u32[]{:S(2)}) collective-permute-start(f32[2,12,40,128]{3,2,1,0:T(8,128)S(1)} %all_to_all.5), channel_id=1, source_target_pairs={{0,16},{2,18},{4,20},{6,22},{8,24},{10,26},{12,28},{14,30},{16,0},... | collective-permute-start | bytes 1474568 | tf_op jit(solution)/shard_map/ppermute | solution.py:25
where the time goes:
time: 98.9 us; the launch traced here: 98.3 us
  waiting for transfers between devices  32.1 us (32%)
  other arithmetic  19.8 us (20%)
  starting transfers between devices  18.6 us (19%)
  local copies, waits for them, and re-layouts  17.7 us (18%)
  blocking collectives  8.79 us (9%)
    ppermute x1, waiting for transfers between devices, from_behind(): lax.ppermute(array, axis, [(i, (i + by) % devices) for i in range(devices)])  18.5 us
    ppermute x6, starting transfers between devices, with_halo(): lax.ppermute(lax.slice_in_dim(block, 0, width, axis=dim), axis, backward)  16.3 us
    all_to_all x1, blocking collectives, per_device(): lax.all_to_all(sendbuf, 'io', split_axis=0, concat_axis=0, tiled=True)  8.79 us
    ppermute x6, waiting for transfers between devices, with_halo(): lax.ppermute(lax.slice_in_dim(block, 0, width, axis=dim), axis, backward)  6.84 us
    ppermute x6, waiting for transfers between devices, with_halo(): lax.ppermute(lax.slice_in_dim(block, block.shape[dim] - width, None, axis...  6.7 us
    mul x3, other arithmetic, advance(): north_open * (jnp.maximum(flow_n, 0.0) * here_n + jnp.minimum(flow_n, 0.0...  6.24 us
    scatter x1, local copies, waits for them, and re-layouts, pack_blocks(): packed = jnp.zeros((levels, total + 1), jnp.float32).at[:, target].set(de...  5.95 us
    slice x5, local copies, waits for them, and re-layouts, with_halo(): lax.slice_in_dim(block, block.shape[dim] - width, None, axis=dim)  3.65 us
  transfers between devices with their start and end apart: 13, of which 7 were waited for; matrix products, arithmetic and copies ran while one was open for 14% of the time, Pallas kernels for 0%

commit v1 on v0

v1 whole, which is shorter than its diff:
```python
import functools
import jax
import jax.numpy as jnp
from jax import lax
from jax.experimental import pallas as pl
from jax.experimental.pallas import tpu as pltpu
from jax.sharding import PartitionSpec as P

MESH = pl.DeviceIdType.MESH
F32 = jnp.float32
BF16 = jnp.bfloat16


def kernel(cap, chunks, tracer, anchor, eflow, nflow, diff, mask, dest,
           out, restart, partner,
           f0, anc, ae, an, dd, be, bn, f1, mi, mf,
           east_s, west_s, east_r, west_r, north_s, south_s, north_r, south_r,
           packed, slots, slots2, table_v, table_p, table_s, table_ps,
           load_sem, table_sem, hs, hr, ps, pr, xs, xr, ys, yr, *got):
    n_comp, n_io = lax.axis_size("comp"), lax.axis_size("io")
    c, a = lax.axis_index("comp"), lax.axis_index("io")
    levels, rows, cols = tracer.shape
    east, west = lax.rem(c + 1, n_comp), lax.rem(c + n_comp - 1, n_comp)
    mate = lax.rem(c + n_comp // 2, n_comp)
    has_north, has_south = a < n_io - 1, a > 0

    zero = jnp.zeros((levels, cols), F32)
    for ref in (north_r, south_r):
        for k in range(3):
            ref[k] = zero

    barrier = pltpu.get_barrier_semaphore()
    for other in (east, west, mate):
        pl.semaphore_signal(barrier, inc=1, device_id={"comp": other}, device_id_type=MESH)
    for t in range(1, n_io):
        pl.semaphore_signal(barrier, inc=1, device_id={"io": lax.rem(a + t, n_io)}, device_id_type=MESH)

    loads = []
    mask_load = pltpu.make_async_copy(mask, mi, load_sem.at[5, 0])
    mask_load.start()
    for k, (src, dst) in enumerate(((tracer, f0), (eflow, ae), (nflow, an), (diff, dd), (anchor, anc))):
        for r in range(rows):
            cp = pltpu.make_async_copy(src.at[:, r, :], dst.at[r], load_sem.at[k, r])
            cp.start()
            loads.append(cp)

    lane = lax.broadcasted_iota(jnp.int32, (levels, cols), 1)
    packed[rows] = zero
    for ref in got:
        ref[rows] = zero[:levels // chunks]

    mask_load.wait()
    mf[...] = mi[...].astype(F32)
    m = mf[...]
    mb = m.astype(BF16)
    qi = lax.broadcasted_iota(jnp.int32, (cols, cols), 0)
    qj = lax.broadcasted_iota(jnp.int32, (cols, cols), 1)
    ki = lax.broadcasted_iota(jnp.int32, (rows, rows), 0)
    kj = lax.broadcasted_iota(jnp.int32, (rows, rows), 1)
    upto = jnp.where(qi <= qj, 1.0, 0.0).astype(BF16)
    before = jnp.where(kj < ki, 1.0, 0.0).astype(BF16)
    cum = jnp.dot(mb, upto, preferred_element_type=F32)
    tot = jnp.dot(mb, jnp.ones((cols, cols), BF16), preferred_element_type=F32)
    start = jnp.dot(before, tot.astype(BF16), preferred_element_type=F32)
    place = (start + cum - 1.0).astype(jnp.int32)
    place = jnp.where(m > 0.5, place & (cols - 1), -1)
    full_before = jnp.maximum(jnp.ceil(start * (1.0 / cols)) - 1.0, 0.0)
    full_after = jnp.maximum(jnp.ceil((start + tot) * (1.0 / cols)) - 1.0, 0.0)
    fill = start - full_before * cols
    over = full_after > full_before
    kk = lax.broadcasted_iota(jnp.int32, (rows, cols), 0)
    qq = lax.broadcasted_iota(jnp.int32, (rows, cols), 1)
    dvec = jnp.zeros((rows, cols), jnp.int32)
    for k in range(rows):
        dvec = jnp.where(kk == k, dest[k], dvec)
    group = jnp.zeros((rows, cols), jnp.int32)
    for g in range(1, n_io + 1):
        group = group + jnp.where(qq >= g * cap, 1, 0)
    slot = qq - group * cap
    hit = jnp.where(dvec == group, 1.0, 0.0)
    earlier = jnp.dot(before, hit.astype(BF16), preferred_element_type=F32)
    chosen = (dvec == group) & (earlier == slot.astype(F32))
    kq = jnp.min(jnp.where(chosen, kk, 1000).astype(F32), axis=0, keepdims=True)
    where_at = jnp.sum(jnp.where(full_after <= kq, 1.0, 0.0), axis=0, keepdims=True) - 1.0
    where_at = where_at + jnp.where(kq > full_after[rows - 1:rows], 1.0, 0.0)
    table_v[...] = jnp.broadcast_to(where_at.astype(jnp.int32), table_v.shape)
    table_load = pltpu.make_async_copy(table_v, table_s, table_sem.at[0])
    table_load.start()

    for cp in loads[:4 * rows]:
        cp.wait()

    for r in range(rows):
        mr = m[r:r + 1]
        u, v, d = ae[r], an[r], dd[r]
        ae[r] = mr * (jnp.maximum(u, 0.0) + d)
        be[r] = mr * (jnp.minimum(u, 0.0) - d)
        an[r] = mr * (jnp.maximum(v, 0.0) + d)
        bn[r] = mr * (jnp.minimum(v, 0.0) - d)

    last = cols - 1
    acc_e, acc_w = zero, zero
    for r in range(rows):
        acc_e = jnp.where(lane == r, (ae[r] * f0[r])[:, last:], acc_e)
        acc_e = jnp.where(lane == rows + r, be[r][:, last:], acc_e)
        acc_w = jnp.where(lane == r, f0[r][:, :1], acc_w)
        acc_w = jnp.where(lane == rows + r, jnp.broadcast_to(m[r:r + 1, :1], (levels, 1)), acc_w)
    east_s[0] = acc_e
    west_s[0] = acc_w
    north_s[0] = an[rows - 1] * f0[rows - 1]
    north_s[1] = bn[rows - 1]
    south_s[0] = f0[0]
    south_s[1] = jnp.broadcast_to(m[0:1], (levels, cols))

    pl.semaphore_wait(barrier, 3 + n_io - 1)

    def halo(step):
        where = slice(0, 2) if step == 0 else slice(2, 3)
        sel = pl.ds(where.start, where.stop - where.start)
        moves = [
            pltpu.make_async_remote_copy(east_s.at[step], east_r.at[step], hs.at[step, 0], hr.at[step, 0],
                                         device_id={"comp": east}, device_id_type=MESH),
            pltpu.make_async_remote_copy(west_s.at[step], west_r.at[step], hs.at[step, 1], hr.at[step, 1],
                                         device_id={"comp": west}, device_id_type=MESH),
        ]
        up = pltpu.make_async_remote_copy(north_s.at[sel], north_r.at[sel], hs.at[step, 2], hr.at[step, 2],
                                          device_id={"io": jnp.minimum(a + 1, n_io - 1)}, device_id_type=MESH)
        down = pltpu.make_async_remote_copy(south_s.at[sel], south_r.at[sel], hs.at[step, 3], hr.at[step, 3],
                                            device_id={"io": jnp.maximum(a - 1, 0)}, device_id_type=MESH)
        return moves, up, down

    def send_halo(step):
        moves, up, down = halo(step)
        for mv in moves:
            mv.start()
        pl.when(has_north)(up.start)
        pl.when(has_south)(down.start)

    def wait_halo(step):
        moves, up, down = halo(step)
        for mv in moves:
            mv.wait()

        @pl.when(has_north)
        def _():
            up.wait_send()
            down.wait_recv()

        @pl.when(has_south)
        def _():
            down.wait_send()
            up.wait_recv()

    send_halo(0)
    table_move = pltpu.make_async_remote_copy(table_v, table_p, ps.at[chunks], pr.at[chunks],
                                              device_id={"comp": mate}, device_id_type=MESH)
    table_move.start()
    wait_halo(0)

    west_0 = west_r[0]
    for r in range(rows):
        me = jnp.where(lane == last, west_0[:, rows + r:rows + r + 1], pltpu.roll(jnp.broadcast_to(m[r:r + 1], (levels, cols)), last, 1))
        ae[r] = ae[r] * me
        be[r] = be[r] * me
        mn = m[r + 1:r + 2] if r < rows - 1 else south_r[1]
        an[r] = an[r] * mn
        bn[r] = bn[r] * mn

    def row_of(step, src, r, fn_below):
        f = src[r]
        e_r, w_r = east_r[step], west_r[step]
        fe = jnp.where(lane == last, w_r[:, r:r + 1], pltpu.roll(f, last, 1))
        flux = ae[r] * f + be[r] * fe
        edge = m[r:r + 1] * (e_r[:, r:r + 1] + east_r[0][:, rows + r:rows + r + 1] * f)
        flux_w = jnp.where(lane == 0, edge, pltpu.roll(flux, 1, 1))
        fn = src[r + 1] if r < rows - 1 else south_r[0 if step == 0 else 2]
        flux_n = an[r] * f + bn[r] * fn
        return f - (flux - flux_w) - (flux_n - fn_below), flux_n

    flux_n = m[0:1] * (north_r[0] + north_r[1] * f0[0])
    acc_e, acc_w = zero, zero
    for r in range(rows):
        new, flux_n = row_of(0, f0, r, flux_n)
        f1[r] = new
        acc_e = jnp.where(lane == r, (ae[r] * new)[:, last:], acc_e)
        acc_w = jnp.where(lane == r, new[:, :1], acc_w)
        if r == 0:
            south_s[2] = new
        if r == rows - 1:
            north_s[2] = an[r] * new
    east_s[1] = acc_e
    west_s[1] = acc_w
    send_halo(1)
    for cp in loads[4 * rows:]:
        cp.wait()
    wait_halo(1)

    flux_n = m[0:1] * (north_r[2] + north_r[1] * f1[0])
    sub = lax.broadcasted_iota(jnp.int32, (cols, cols), 0)
    acc = zero
    outs = []
    for r in range(rows):
        new, flux_n = row_of(1, f1, r, flux_n)
        f0[r] = new
        delta = new - anc[r]
        hi = delta.astype(BF16).astype(F32)
        mid = (delta - hi).astype(BF16).astype(F32)
        low = delta - hi - mid
        parts = jnp.concatenate([hi, mid, low], axis=0).astype(BF16)
        pick = jnp.where(sub == place[r:r + 1], 1.0, 0.0).astype(BF16)
        got_r = lax.dot_general(parts, pick, (((1,), (1,)), ((), ())), preferred_element_type=F32)
        row = got_r[:levels] + got_r[levels:2 * levels] + got_r[2 * levels:]
        lanef = lane.astype(F32)
        begins = fill[r:r + 1]
        now = acc + jnp.where(lanef >= begins, row, 0.0)
        if r > 0:
            packed[r - 1] = now
        crossed = jnp.broadcast_to(jnp.where(over[r:r + 1], 1.0, 0.0), (levels, cols)) > 0.5
        acc = jnp.where(crossed, jnp.where(lanef < begins, row, 0.0), now)
    packed[rows - 1] = acc

    for r in range(rows):
        cp = pltpu.make_async_copy(f0.at[r], out.at[:, r, :], load_sem.at[0, r])
        cp.start()
        outs.append(cp)

    step_l = levels // chunks
    to_mate = []
    for k in range(chunks):
        part = pl.ds(k * step_l, step_l)
        cp = pltpu.make_async_remote_copy(packed.at[pl.ds(0, rows), part], got[k].at[pl.ds(0, rows)], ps.at[k], pr.at[k],
                                          device_id={"comp": mate}, device_id_type=MESH)
        cp.start()
        to_mate.append(cp)

    table_load.wait()
    pending = []
    for t in range(1, n_io):
        g = lax.rem(a + t, n_io)
        for s in range(cap):
            slots[t - 1, s] = packed[jnp.clip(table_s[0, g * cap + s], 0, rows)]
        cp = pltpu.make_async_remote_copy(slots.at[t - 1], restart.at[a], xs.at[t], xr.at[t],
                                          device_id={"io": g}, device_id_type=MESH)
        cp.start()
        pending.append(cp)
    for s in range(cap):
        restart[a, s] = packed[jnp.clip(table_s[0, a * cap + s], 0, rows)]

    table_move.wait()
    table_load = pltpu.make_async_copy(table_p, table_ps, table_sem.at[1])
    table_load.start()
    table_load.wait()
    for k in range(chunks):
        part = pl.ds(k * step_l, step_l)
        to_mate[k].wait_recv()
        for t in range(1, n_io):
            g = lax.rem(a + t, n_io)
            for s in range(cap):
                slots2[t - 1, s, part] = got[k][jnp.clip(table_ps[0, g * cap + s], 0, rows)]
            cp = pltpu.make_async_remote_copy(slots2.at[t - 1, :, part], partner.at[a, :, part], ys.at[t, k], yr.at[t, k],
                                              device_id={"io": g}, device_id_type=MESH)
            cp.start()
            pending.append(cp)
        for s in range(cap):
            partner[a, s, part] = got[k][jnp.clip(table_ps[0, a * cap + s], 0, rows)]
    for cp in to_mate:
        cp.wait_send()
    for cp in pending:
        cp.wait_send()
    for t in range(1, n_io):
        g = lax.rem(a + n_io - t, n_io)
        pltpu.make_async_remote_copy(slots.at[t - 1], restart.at[g], xs.at[t], xr.at[t],
                                     device_id={"io": lax.rem(a + t, n_io)}, device_id_type=MESH).wait_recv()
        for k in range(chunks):
            part = pl.ds(k * step_l, step_l)
            pltpu.make_async_remote_copy(slots2.at[t - 1, :, part], partner.at[g, :, part], ys.at[t, k], yr.at[t, k],
                                         device_id={"io": lax.rem(a + t, n_io)}, device_id_type=MESH).wait_recv()
    for cp in outs:
        cp.wait()


def per_device(tracer, anchor, east_flow, north_flow, diffusivity, land_mask, block_dest):
    n_io = lax.axis_size("io")
    levels, rows, cols = tracer.shape
    cap = max(2, 3 * rows // (2 * n_io))
    chunks = 5
    tile = pltpu.VMEM((rows, levels, cols), F32)
    dma = pltpu.SemaphoreType.DMA
    return pl.pallas_call(
        functools.partial(kernel, cap, chunks),
        out_shape=(
            jax.ShapeDtypeStruct((levels, rows, cols), F32),
            jax.ShapeDtypeStruct((n_io, cap, levels, cols), F32),
            jax.ShapeDtypeStruct((n_io, cap, levels, cols), F32),
        ),
        in_specs=[pl.BlockSpec(memory_space=pl.ANY)] * 6 + [pl.BlockSpec(memory_space=pltpu.SMEM)],
        out_specs=(
            pl.BlockSpec(memory_space=pl.ANY),
            pl.BlockSpec(memory_space=pltpu.VMEM),
            pl.BlockSpec(memory_space=pltpu.VMEM),
        ),
        scratch_shapes=[tile] * 8 + [pltpu.VMEM((rows, cols), jnp.int32), pltpu.VMEM((rows, cols), F32)]
        + [pltpu.VMEM((2, levels, cols), F32)] * 4
        + [pltpu.VMEM((3, levels, cols), F32)] * 4
        + [pltpu.VMEM((rows + 1, levels, cols), F32)]
        + [pltpu.VMEM((max(n_io - 1, 1), cap, levels, cols), F32)] * 2
        + [pltpu.VMEM((8, cols), jnp.int32)] * 2
        + [pltpu.SMEM((8, cols), jnp.int32)] * 2
        + [dma((6, rows)), dma((2,)), dma((2, 4)), dma((2, 4)), dma((chunks + 1,)), dma((chunks + 1,)),
           dma((n_io,)), dma((n_io,)), dma((n_io, chunks)), dma((n_io, chunks))]
        + [pltpu.VMEM((rows + 1, levels // chunks, cols), F32)] * chunks,
        compiler_params=pltpu.CompilerParams(collective_id=0, has_side_effects=True, vmem_limit_bytes=48 * 1024 * 1024),
        name="tracer_restart",
    )(tracer, anchor, east_flow, north_flow, diffusivity, land_mask, block_dest.reshape(rows))


def solution(mesh):
    placed = (
        P(None, "io", "comp"),
        P(None, "io", "comp"),
        P(None, "io", "comp"),
        P(None, "io", "comp"),
        P(None, "io", "comp"),
        P("io", "comp"),
        P("comp", "io", None),
    )
    return jax.shard_map(
        per_device,
        mesh=mesh,
        in_specs=placed,
        out_specs=(P(None, "io", "comp"), P("io", None, None, "comp"), P("io", None, None, "comp")),
        check_vma=False,
    )
```

time: 98.9 us -> 45.9 us (0.46)
  Pallas kernels: 0 us -> 36.5 us
  waiting for transfers between devices: 32.1 us -> 0 us
  other arithmetic: 19.8 us -> 0 us
  starting transfers between devices: 18.6 us -> 0 us
  local copies, waits for them, and re-layouts: 17.7 us -> 8.49 us
  blocking collectives: 8.79 us -> 0 us
    pallas_call x0 -> x1, Pallas kernels: none -> 36.5 us  [per_device(): pl.pallas_call(functools.partial(kernel, cap, chunks), out_shape=(jax.Sha...]
    ppermute x13 -> x0, waiting for transfers between devices: 32.1 us -> none  [the longest x1 18.5 us: from_behind(): lax.ppermute(array, axis, [(i, (i + by) % devices) for i in range(devices)])]
    ppermute x13 -> x0, starting transfers between devices: 18.6 us -> none  [the longest x6 16.3 us: with_halo(): lax.ppermute(lax.slice_in_dim(block, 0, width, axis=dim), axis, backward)]
    all_to_all x1 -> x0, blocking collectives: 8.79 us -> none  [per_device(): lax.all_to_all(sendbuf, 'io', split_axis=0, concat_axis=0, tiled=True)]
    mul x6 -> x0, other arithmetic: 7.24 us -> none  [the longest x3 6.24 us: advance(): north_open * (jnp.maximum(flow_n, 0.0) * here_n + jnp.minimum(flow_n, 0.0...]
    scatter x1 -> x0, local copies, waits for them, and re-layouts: 5.95 us -> none  [pack_blocks(): packed = jnp.zeros((levels, total + 1), jnp.float32).at[:, target].set(de...]
    unnamed x24 -> x17, local copies, waits for them, and re-layouts: 2.75 us -> 8.49 us
    slice x9 -> x0, local copies, waits for them, and re-layouts: 4.97 us -> none  [the longest x5 3.65 us: with_halo(): lax.slice_in_dim(block, block.shape[dim] - width, None, axis=dim)]
  transfers between devices with their start and end apart: 13 -> 0, of which waited for: 7 -> 0; matrix products, arithmetic and copies ran while one was open for 14% -> 0% of each run, Pallas kernels for 0% -> 0%
where the time goes in v1:
time: 45.9 us; the launch traced here: 45.6 us
  Pallas kernels  36.5 us (80%)
  local copies, waits for them, and re-layouts  8.49 us (18%)
  between operations  0.66 us (1%)
    pallas_call x1, Pallas kernels, per_device(): pl.pallas_call(functools.partial(kernel, cap, chunks), out_shape=(jax.Sha...  36.5 us
    unnamed x17, local copies, waits for them, and re-layouts  8.49 us

profile of v1, /device:TPU:0, one launch (start us, length us, event | category | flops | bytes accessed | tf_op | source)
XLA Modules:
  0.0 45.6 jit_solution(1650303720221379573)
XLA Ops:
  0.6 0.0 copy-start.6
  0.6 0.6 %copy-done.6 = s32[1,16,1]{1,2,0:T(1,128)S(1)} copy-done((s32[1,16,1]{1,2,0:T(1,128)S(1)}, s32[1,16,1]{1,2,0:T(1,128)}, u32[]{:S(2)}) %copy-start.6) | copy-done | bytes 88
  1.3 0.0 copy-start
  1.3 1.0 %copy-done = f32[40,16,128]{2,1,0:T(8,128)S(1)} copy-done((f32[40,16,128]{2,1,0:T(8,128)S(1)}, f32[40,16,128]{2,1,0:T(8,128)}, u32[]{:S(2)}) %copy-start) | copy-done | bytes 327704
  2.3 0.0 copy-start.1
  2.3 1.0 %copy-done.1 = f32[40,16,128]{2,1,0:T(8,128)S(1)} copy-done((f32[40,16,128]{2,1,0:T(8,128)S(1)}, f32[40,16,128]{2,1,0:T(8,128)}, u32[]{:S(2)}) %copy-start.1) | copy-done | bytes 327704
  3.2 0.0 copy-start.2
  3.2 1.0 %copy-done.2 = f32[40,16,128]{2,1,0:T(8,128)S(1)} copy-done((f32[40,16,128]{2,1,0:T(8,128)S(1)}, f32[40,16,128]{2,1,0:T(8,128)}, u32[]{:S(2)}) %copy-start.2) | copy-done | bytes 327704
  4.2 0.0 copy-start.3
  4.2 1.0 %copy-done.3 = f32[40,16,128]{2,1,0:T(8,128)S(1)} copy-done((f32[40,16,128]{2,1,0:T(8,128)S(1)}, f32[40,16,128]{2,1,0:T(8,128)}, u32[]{:S(2)}) %copy-start.3) | copy-done | bytes 327704
  5.2 0.0 copy-start.4
  5.2 1.0 %copy-done.4 = f32[40,16,128]{2,1,0:T(8,128)S(1)} copy-done((f32[40,16,128]{2,1,0:T(8,128)S(1)}, f32[40,16,128]{2,1,0:T(8,128)}, u32[]{:S(2)}) %copy-start.4) | copy-done | bytes 327704
  6.2 0.0 copy-start.5
  6.2 0.7 %copy-done.5 = s32[16,128]{1,0:T(8,128)S(1)} copy-done((s32[16,128]{1,0:T(8,128)S(1)}, s32[16,128]{1,0:T(8,128)}, u32[]{:S(2)}) %copy-start.5) | copy-done | bytes 8216
  6.9 36.5 %tracer_restart.1 = (f32[40,16,128]{2,1,0:T(8,128)S(1)}, f32[2,12,40,128]{3,2,1,0:T(8,128)S(1)}, f32[2,12,40,128]{3,2,1,0:T(8,128)S(1)}) custom-call(f32[40,16,128]{2,1,0:T(8,128)S(1)} %copy-done, f32[40,16,128]{2,1,0:T(8,128)S(1)} %copy-done.1, f32[40,16,128]{2,1,0:T(8,128)S(1)} %copy-done.2, f32[40,16,128]{2,1,0:T(8,128)S(1)} %copy-done.3, ...), custom_call_target="tpu_custom_call" | custom-call | tf_op jit(solution)/shard_map/tracer_restart/pallas_call | solution.py:289
  43.3 0.7 %copy.13 = f32[40,16,128]{2,1,0:T(8,128)} copy(f32[40,16,128]{2,1,0:T(8,128)S(1)} %get-tuple-element.6) | data formatting | bytes 655360
  44.0 0.8 %copy.14 = f32[2,12,40,128]{3,2,1,0:T(8,128)} copy(f32[2,12,40,128]{3,2,1,0:T(8,128)S(1)} %get-tuple-element.7) | data formatting | bytes 983040
  44.8 0.8 %copy.15 = f32[2,12,40,128]{3,2,1,0:T(8,128)} copy(f32[2,12,40,128]{3,2,1,0:T(8,128)S(1)} %get-tuple-element.8) | data formatting | bytes 983040
Async XLA Ops:
  0.6 0.7 %copy-start.6 = (s32[1,16,1]{1,2,0:T(1,128)S(1)}, s32[1,16,1]{1,2,0:T(1,128)}, u32[]{:S(2)}) copy-start(s32[1,16,1]{1,2,0:T(1,128)} %param.13) | copy-start | bytes 196
  1.3 1.0 %copy-start = (f32[40,16,128]{2,1,0:T(8,128)S(1)}, f32[40,16,128]{2,1,0:T(8,128)}, u32[]{:S(2)}) copy-start(f32[40,16,128]{2,1,0:T(8,128)} %tracer.1) | copy-start | bytes 983044
  2.3 1.0 %copy-start.1 = (f32[40,16,128]{2,1,0:T(8,128)S(1)}, f32[40,16,128]{2,1,0:T(8,128)}, u32[]{:S(2)}) copy-start(f32[40,16,128]{2,1,0:T(8,128)} %anchor.1) | copy-start | bytes 983044
  3.2 1.0 %copy-start.2 = (f32[40,16,128]{2,1,0:T(8,128)S(1)}, f32[40,16,128]{2,1,0:T(8,128)}, u32[]{:S(2)}) copy-start(f32[40,16,128]{2,1,0:T(8,128)} %eflow.1) | copy-start | bytes 983044
  4.2 1.0 %copy-start.3 = (f32[40,16,128]{2,1,0:T(8,128)S(1)}, f32[40,16,128]{2,1,0:T(8,128)}, u32[]{:S(2)}) copy-start(f32[40,16,128]{2,1,0:T(8,128)} %nflow.1) | copy-start | bytes 983044
  5.2 1.0 %copy-start.4 = (f32[40,16,128]{2,1,0:T(8,128)S(1)}, f32[40,16,128]{2,1,0:T(8,128)}, u32[]{:S(2)}) copy-start(f32[40,16,128]{2,1,0:T(8,128)} %diff.1) | copy-start | bytes 983044
  6.2 0.7 %copy-start.5 = (s32[16,128]{1,0:T(8,128)S(1)}, s32[16,128]{1,0:T(8,128)}, u32[]{:S(2)}) copy-start(s32[16,128]{1,0:T(8,128)} %mask.1) | copy-start | bytes 24580

commit v2 on v1

--- a/solution.py
+++ b/solution.py
@@ -202,6 +202,9 @@
     for r in range(rows):
         new, flux_n = row_of(1, f1, r, flux_n)
         f0[r] = new
+        cp = pltpu.make_async_copy(f0.at[r], out.at[:, r, :], load_sem.at[0, r])
+        cp.start()
+        outs.append(cp)
         delta = new - anc[r]
         hi = delta.astype(BF16).astype(F32)
         mid = (delta - hi).astype(BF16).astype(F32)
@@ -219,11 +222,6 @@
         acc = jnp.where(crossed, jnp.where(lanef < begins, row, 0.0), now)
     packed[rows - 1] = acc
 
-    for r in range(rows):
-        cp = pltpu.make_async_copy(f0.at[r], out.at[:, r, :], load_sem.at[0, r])
-        cp.start()
-        outs.append(cp)
-
     step_l = levels // chunks
     to_mate = []
     for k in range(chunks):
@@ -244,7 +242,11 @@
         cp.start()
         pending.append(cp)
     for s in range(cap):
-        restart[a, s] = packed[jnp.clip(table_s[0, a * cap + s], 0, rows)]
+        slots[n_io - 1, s] = packed[jnp.clip(table_s[0, a * cap + s], 0, rows)]
+
+    cp = pltpu.make_async_copy(slots.at[n_io - 1], restart.at[a], load_sem.at[1, 0])
+    cp.start()
+    outs.append(cp)
 
     table_move.wait()
     table_load = pltpu.make_async_copy(table_p, table_ps, table_sem.at[1])
@@ -262,7 +264,10 @@
             cp.start()
             pending.append(cp)
         for s in range(cap):
-            partner[a, s, part] = got[k][jnp.clip(table_ps[0, a * cap + s], 0, rows)]
+            slots2[n_io - 1, s, part] = got[k][jnp.clip(table_ps[0, a * cap + s], 0, rows)]
+        cp = pltpu.make_async_copy(slots2.at[n_io - 1, :, part], partner.at[a, :, part], load_sem.at[2, k])
+        cp.start()
+        outs.append(cp)
     for cp in to_mate:
         cp.wait_send()
     for cp in pending:
@@ -296,20 +301,20 @@
         in_specs=[pl.BlockSpec(memory_space=pl.ANY)] * 6 + [pl.BlockSpec(memory_space=pltpu.SMEM)],
         out_specs=(
             pl.BlockSpec(memory_space=pl.ANY),
-            pl.BlockSpec(memory_space=pltpu.VMEM),
-            pl.BlockSpec(memory_space=pltpu.VMEM),
+            pl.BlockSpec(memory_space=pl.ANY),
+            pl.BlockSpec(memory_space=pl.ANY),
         ),
         scratch_shapes=[tile] * 8 + [pltpu.VMEM((rows, cols), jnp.int32), pltpu.VMEM((rows, cols), F32)]
         + [pltpu.VMEM((2, levels, cols), F32)] * 4
         + [pltpu.VMEM((3, levels, cols), F32)] * 4
         + [pltpu.VMEM((rows + 1, levels, cols), F32)]
-        + [pltpu.VMEM((max(n_io - 1, 1), cap, levels, cols), F32)] * 2
+        + [pltpu.VMEM((n_io, cap, levels, cols), F32)] * 2
         + [pltpu.VMEM((8, cols), jnp.int32)] * 2
         + [pltpu.SMEM((8, cols), jnp.int32)] * 2
         + [dma((6, rows)), dma((2,)), dma((2, 4)), dma((2, 4)), dma((chunks + 1,)), dma((chunks + 1,)),
            dma((n_io,)), dma((n_io,)), dma((n_io, chunks)), dma((n_io, chunks))]
         + [pltpu.VMEM((rows + 1, levels // chunks, cols), F32)] * chunks,
-        compiler_params=pltpu.CompilerParams(collective_id=0, has_side_effects=True, vmem_limit_bytes=48 * 1024 * 1024),
+        compiler_params=pltpu.CompilerParams(collective_id=0, has_side_effects=True),
         name="tracer_restart",
     )(tracer, anchor, east_flow, north_flow, diffusivity, land_mask, block_dest.reshape(rows))
 

time: 45.9 us -> 41.1 us (0.90)
  local copies, waits for them, and re-layouts: 8.49 us -> 3.76 us
    unnamed x17 -> x7, local copies, waits for them, and re-layouts: 8.49 us -> 3.76 us
where the time goes in v2:
time: 41.1 us; the launch traced here: 40.7 us
  Pallas kernels  36.3 us (88%)
  local copies, waits for them, and re-layouts  3.76 us (9%)
  between operations  0.65 us (2%)
    pallas_call x1, Pallas kernels, per_device(): pl.pallas_call(functools.partial(kernel, cap, chunks), out_shape=(jax.Sha...  36.3 us
    unnamed x7, local copies, waits for them, and re-layouts  3.76 us

profile of v2, /device:TPU:0, one launch (start us, length us, event | category | flops | bytes accessed | tf_op | source)
XLA Modules:
  0.0 40.7 jit_solution(4332465018708020122)
XLA Ops:
  0.6 36.3 %tracer_restart.1 = (f32[40,16,128]{2,1,0:T(8,128)}, f32[2,12,40,128]{3,2,1,0:T(8,128)}, f32[2,12,40,128]{3,2,1,0:T(8,128)}) custom-call(f32[40,16,128]{2,1,0:T(8,128)} %tracer.1, f32[40,16,128]{2,1,0:T(8,128)} %anchor.1, f32[40,16,128]{2,1,0:T(8,128)} %eflow.1, f32[40,16,128]{2,1,0:T(8,128)} %nflow.1, f32[40,16,128]{2,1,0:T(8,128)} %diff.1, ...), custom_call_target="tpu_custom_call" | custom-call | tf_op jit(solution)/shard_map/tracer_restart/pallas_call | solution.py:294
  37.0 0.0 copy-start.1
  37.0 1.8 %copy.13 = f32[40,16,128]{2,1,0:T(8,128)} copy(f32[40,16,128]{2,1,0:T(8,128)} %get-tuple-element.6) | data formatting | bytes 655360
  38.8 0.0 copy-done.1
  38.8 0.0 copy-start
  38.8 0.8 %copy.14 = f32[2,12,40,128]{3,2,1,0:T(8,128)} copy(f32[2,12,40,128]{3,2,1,0:T(8,128)S(1)} %copy-done.1) | data formatting | bytes 983040
  39.5 0.4 %copy-done = f32[2,12,40,128]{3,2,1,0:T(8,128)S(1)} copy-done((f32[2,12,40,128]{3,2,1,0:T(8,128)S(1)}, f32[2,12,40,128]{3,2,1,0:T(8,128)}, u32[]{:S(2)}) %copy-start) | copy-done | bytes 491544
  40.0 0.8 %copy.15 = f32[2,12,40,128]{3,2,1,0:T(8,128)} copy(f32[2,12,40,128]{3,2,1,0:T(8,128)S(1)} %copy-done) | data formatting | bytes 983040
Async XLA Ops:
  37.0 1.8 %copy-start.1 = (f32[2,12,40,128]{3,2,1,0:T(8,128)S(1)}, f32[2,12,40,128]{3,2,1,0:T(8,128)}, u32[]{:S(2)}) copy-start(f32[2,12,40,128]{3,2,1,0:T(8,128)} %get-tuple-element.7) | copy-start | bytes 1474564
  38.8 1.2 %copy-start = (f32[2,12,40,128]{3,2,1,0:T(8,128)S(1)}, f32[2,12,40,128]{3,2,1,0:T(8,128)}, u32[]{:S(2)}) copy-start(f32[2,12,40,128]{3,2,1,0:T(8,128)} %get-tuple-element.8) | copy-start | bytes 1474564

commit v3 on v2

--- a/solution.py
+++ b/solution.py
@@ -15,7 +15,7 @@
            out, restart, partner,
            f0, anc, ae, an, dd, be, bn, f1, mi, mf,
            east_s, west_s, east_r, west_r, north_s, south_s, north_r, south_r,
-           packed, slots, slots2, table_v, table_p, table_s, table_ps,
+           packed, early, bulk_r, edges, edges_r, picks, mfp, slots, slots2, table_v, table_p, table_s, table_ps,
            load_sem, table_sem, hs, hr, ps, pr, xs, xr, ys, yr, *got):
     n_comp, n_io = lax.axis_size("comp"), lax.axis_size("io")
     c, a = lax.axis_index("comp"), lax.axis_index("io")
@@ -23,6 +23,7 @@
     east, west = lax.rem(c + 1, n_comp), lax.rem(c + n_comp - 1, n_comp)
     mate = lax.rem(c + n_comp // 2, n_comp)
     has_north, has_south = a < n_io - 1, a > 0
+    first = 4
 
     zero = jnp.zeros((levels, cols), F32)
     for ref in (north_r, south_r):
@@ -52,22 +53,25 @@
     mask_load.wait()
     mf[...] = mi[...].astype(F32)
     m = mf[...]
-    mb = m.astype(BF16)
     qi = lax.broadcasted_iota(jnp.int32, (cols, cols), 0)
     qj = lax.broadcasted_iota(jnp.int32, (cols, cols), 1)
     ki = lax.broadcasted_iota(jnp.int32, (rows, rows), 0)
     kj = lax.broadcasted_iota(jnp.int32, (rows, rows), 1)
     upto = jnp.where(qi <= qj, 1.0, 0.0).astype(BF16)
     before = jnp.where(kj < ki, 1.0, 0.0).astype(BF16)
-    cum = jnp.dot(mb, upto, preferred_element_type=F32)
-    tot = jnp.dot(mb, jnp.ones((cols, cols), BF16), preferred_element_type=F32)
-    start = jnp.dot(before, tot.astype(BF16), preferred_element_type=F32)
-    place = (start + cum - 1.0).astype(jnp.int32)
-    place = jnp.where(m > 0.5, place & (cols - 1), -1)
-    full_before = jnp.maximum(jnp.ceil(start * (1.0 / cols)) - 1.0, 0.0)
-    full_after = jnp.maximum(jnp.ceil((start + tot) * (1.0 / cols)) - 1.0, 0.0)
-    fill = start - full_before * cols
-    over = full_after > full_before
+
+    def places(m):
+        mb = m.astype(BF16)
+        cum = jnp.dot(mb, upto, preferred_element_type=F32)
+        tot = jnp.dot(mb, jnp.ones((cols, cols), BF16), preferred_element_type=F32)
+        start = jnp.dot(before, tot.astype(BF16), preferred_element_type=F32)
+        place = (start + cum - 1.0).astype(jnp.int32)
+        place = jnp.where(m > 0.5, place & (cols - 1), -1)
+        full_before = jnp.maximum(jnp.ceil(start * (1.0 / cols)) - 1.0, 0.0)
+        full_after = jnp.maximum(jnp.ceil((start + tot) * (1.0 / cols)) - 1.0, 0.0)
+        return place, start - full_before * cols, jnp.where(full_after > full_before, 1.0, 0.0), full_after
+
+    place, fill, over, full_after = places(m)
     kk = lax.broadcasted_iota(jnp.int32, (rows, cols), 0)
     qq = lax.broadcasted_iota(jnp.int32, (rows, cols), 1)
     dvec = jnp.zeros((rows, cols), jnp.int32)
@@ -87,7 +91,7 @@
     table_load = pltpu.make_async_copy(table_v, table_s, table_sem.at[0])
     table_load.start()
 
-    for cp in loads[:4 * rows]:
+    for cp in loads:
         cp.wait()
 
     for r in range(rows):
@@ -155,16 +159,50 @@
     table_move = pltpu.make_async_remote_copy(table_v, table_p, ps.at[chunks], pr.at[chunks],
                                               device_id={"comp": mate}, device_id_type=MESH)
     table_move.start()
-    wait_halo(0)
-
-    west_0 = west_r[0]
-    for r in range(rows):
-        me = jnp.where(lane == last, west_0[:, rows + r:rows + r + 1], pltpu.roll(jnp.broadcast_to(m[r:r + 1], (levels, cols)), last, 1))
+    mask_move = pltpu.make_async_remote_copy(mf, mfp, ps.at[chunks + 1], pr.at[chunks + 1],
+                                             device_id={"comp": mate}, device_id_type=MESH)
+    mask_move.start()
+
+    for r in range(rows):
+        me = jnp.where(lane == last, 1.0, pltpu.roll(jnp.broadcast_to(m[r:r + 1], (levels, cols)), last, 1))
         ae[r] = ae[r] * me
         be[r] = be[r] * me
-        mn = m[r + 1:r + 2] if r < rows - 1 else south_r[1]
-        an[r] = an[r] * mn
-        bn[r] = bn[r] * mn
+        if r < rows - 1:
+            an[r] = an[r] * m[r + 1:r + 2]
+            bn[r] = bn[r] * m[r + 1:r + 2]
+
+    def inner(src, r):
+        f = src[r]
+        flux = ae[r] * f + be[r] * pltpu.roll(f, last, 1)
+        return f - (flux - pltpu.roll(flux, 1, 1))
+
+    def north_flux(src, r):
+        return an[r] * src[r] + bn[r] * src[r + 1]
+
+    below = north_flux(f0, 0)
+    for r in range(1, rows - 1):
+        above = north_flux(f0, r)
+        f1[r] = inner(f0, r) - (above - below)
+        below = above
+    below = north_flux(f1, 1)
+    for r in range(2, rows - 2):
+        above = north_flux(f1, r)
+        early[r - 2] = inner(f1, r) - (above - below) - anc[r]
+        below = above
+    cuts = ((0, first), (first, rows - 4 - first))
+    bulk = [pltpu.make_async_remote_copy(early.at[pl.ds(at, many)], bulk_r.at[pl.ds(at, many)], ps.at[chunks + 2 + k],
+                                         pr.at[chunks + 2 + k], device_id={"comp": mate}, device_id_type=MESH)
+            for k, (at, many) in enumerate(cuts)]
+    bulk[0].start()
+
+    wait_halo(0)
+    west_0 = west_r[0]
+    for r in range(rows):
+        me = jnp.where(lane == last, west_0[:, rows + r:rows + r + 1], 1.0)
+        ae[r] = ae[r] * me
+        be[r] = be[r] * me
+    an[rows - 1] = an[rows - 1] * south_r[1]
+    bn[rows - 1] = bn[rows - 1] * south_r[1]
 
     def row_of(step, src, r, fn_below):
         f = src[r]
@@ -191,14 +229,14 @@
     east_s[1] = acc_e
     west_s[1] = acc_w
     send_halo(1)
-    for cp in loads[4 * rows:]:
-        cp.wait()
+    bulk[1].start()
     wait_halo(1)
 
     flux_n = m[0:1] * (north_r[2] + north_r[1] * f1[0])
-    sub = lax.broadcasted_iota(jnp.int32, (cols, cols), 0)
-    acc = zero
     outs = []
+    acc_f = zero
+    edge_rows = (0, 1, rows - 2, rows - 1)
+    edge_cols = (0, 1, cols - 2, cols - 1)
     for r in range(rows):
         new, flux_n = row_of(1, f1, r, flux_n)
         f0[r] = new
@@ -206,30 +244,52 @@
         cp.start()
         outs.append(cp)
         delta = new - anc[r]
-        hi = delta.astype(BF16).astype(F32)
-        mid = (delta - hi).astype(BF16).astype(F32)
-        low = delta - hi - mid
-        parts = jnp.concatenate([hi, mid, low], axis=0).astype(BF16)
-        pick = jnp.where(sub == place[r:r + 1], 1.0, 0.0).astype(BF16)
-        got_r = lax.dot_general(parts, pick, (((1,), (1,)), ((), ())), preferred_element_type=F32)
-        row = got_r[:levels] + got_r[levels:2 * levels] + got_r[2 * levels:]
-        lanef = lane.astype(F32)
-        begins = fill[r:r + 1]
-        now = acc + jnp.where(lanef >= begins, row, 0.0)
-        if r > 0:
-            packed[r - 1] = now
-        crossed = jnp.broadcast_to(jnp.where(over[r:r + 1], 1.0, 0.0), (levels, cols)) > 0.5
-        acc = jnp.where(crossed, jnp.where(lanef < begins, row, 0.0), now)
-    packed[rows - 1] = acc
-
+        anc[r] = delta
+        if r in edge_rows:
+            edges[edge_rows.index(r)] = delta
+        else:
+            for k, col in enumerate(edge_cols):
+                acc_f = jnp.where(lane == k * rows + r, delta[:, col:col + 1], acc_f)
+    edges[4] = acc_f
     step_l = levels // chunks
     to_mate = []
     for k in range(chunks):
         part = pl.ds(k * step_l, step_l)
-        cp = pltpu.make_async_remote_copy(packed.at[pl.ds(0, rows), part], got[k].at[pl.ds(0, rows)], ps.at[k], pr.at[k],
+        cp = pltpu.make_async_remote_copy(edges.at[:, part], edges_r.at[:, part], ps.at[k], pr.at[k],
                                           device_id={"comp": mate}, device_id_type=MESH)
         cp.start()
         to_mate.append(cp)
+
+    sub = lax.broadcasted_iota(jnp.int32, (cols, cols), 0)
+
+    def one_hot(place, r):
+        return jnp.where(sub == place[r:r + 1], 1.0, 0.0).astype(BF16)
+
+    def compact(delta_of, pick_of, fill, over, store):
+        acc = None
+        for r in range(rows):
+            delta = delta_of(r)
+            n = delta.shape[0]
+            hi = delta.astype(BF16).astype(F32)
+            mid = (delta - hi).astype(BF16).astype(F32)
+            low = delta - hi - mid
+            parts = jnp.concatenate([hi, mid, low], axis=0).astype(BF16)
+            moved = lax.dot_general(parts, pick_of(r), (((1,), (1,)), ((), ())), preferred_element_type=F32)
+            row = moved[:n] + moved[n:2 * n] + moved[2 * n:]
+            if r == 0:
+                acc = row
+                continue
+            starts = lax.broadcasted_iota(jnp.int32, (n, cols), 1).astype(F32) >= fill[r:r + 1]
+            now = acc + jnp.where(starts, row, 0.0)
+            store(r - 1, now)
+            crossed = jnp.broadcast_to(over[r:r + 1], (n, cols)) > 0.5
+            acc = jnp.where(crossed, jnp.where(starts, 0.0, row), now)
+        store(rows - 1, acc)
+
+    def keep(r, block):
+        packed[r] = block
+
+    compact(lambda r: anc[r], lambda r: one_hot(place, r), fill, over, keep)
 
     table_load.wait()
     pending = []
@@ -251,10 +311,30 @@
     table_move.wait()
     table_load = pltpu.make_async_copy(table_p, table_ps, table_sem.at[1])
     table_load.start()
+    mask_move.wait()
+    place_p, fill_p, over_p, _ = places(mfp[...])
+    for r in range(rows):
+        picks[r] = one_hot(place_p, r)
     table_load.wait()
+    for cp in bulk:
+        cp.wait()
+    lane_l = lax.broadcasted_iota(jnp.int32, (step_l, cols), 1)
     for k in range(chunks):
         part = pl.ds(k * step_l, step_l)
         to_mate[k].wait_recv()
+
+        def delta_of(r):
+            if r in edge_rows:
+                return edges_r[edge_rows.index(r), part]
+            delta, sides = bulk_r[r - 2, part], edges_r[4, part]
+            for q, col in enumerate(edge_cols):
+                delta = jnp.where(lane_l == col, sides[:, q * rows + r:q * rows + r + 1], delta)
+            return delta
+
+        def keep_p(r, block):
+            got[k][r] = block
+
+        compact(delta_of, lambda r: picks[r], fill_p, over_p, keep_p)
         for t in range(1, n_io):
             g = lax.rem(a + t, n_io)
             for s in range(cap):
@@ -308,10 +388,13 @@
         + [pltpu.VMEM((2, levels, cols), F32)] * 4
         + [pltpu.VMEM((3, levels, cols), F32)] * 4
         + [pltpu.VMEM((rows + 1, levels, cols), F32)]
+        + [pltpu.VMEM((rows - 4, levels, cols), F32)] * 2
+        + [pltpu.VMEM((5, levels, cols), F32)] * 2
+        + [pltpu.VMEM((rows, cols, cols), BF16), pltpu.VMEM((rows, cols), F32)]
         + [pltpu.VMEM((n_io, cap, levels, cols), F32)] * 2
         + [pltpu.VMEM((8, cols), jnp.int32)] * 2
         + [pltpu.SMEM((8, cols), jnp.int32)] * 2
-        + [dma((6, rows)), dma((2,)), dma((2, 4)), dma((2, 4)), dma((chunks + 1,)), dma((chunks + 1,)),
+        + [dma((6, rows)), dma((2,)), dma((2, 4)), dma((2, 4)), dma((chunks + 4,)), dma((chunks + 4,)),
            dma((n_io,)), dma((n_io,)), dma((n_io, chunks)), dma((n_io, chunks))]
         + [pltpu.VMEM((rows + 1, levels // chunks, cols), F32)] * chunks,
         compiler_params=pltpu.CompilerParams(collective_id=0, has_side_effects=True),

time: 41.1 us -> 37.1 us (0.903)
  Pallas kernels: 36.3 us -> 32.3 us
    pallas_call x1, Pallas kernels: 36.3 us -> 32.3 us  [per_device(): pl.pallas_call(functools.partial(kernel, cap, chunks), out_shape=(jax.Sha...]
where the time goes in v3:
time: 37.1 us; the launch traced here: 36.7 us
  Pallas kernels  32.3 us (87%)
  local copies, waits for them, and re-layouts  3.76 us (10%)
  between operations  0.65 us (2%)
    pallas_call x1, Pallas kernels, per_device(): pl.pallas_call(functools.partial(kernel, cap, chunks), out_shape=(jax.Sha...  32.3 us
    unnamed x7, local copies, waits for them, and re-layouts  3.76 us

profile of v3, /device:TPU:0, one launch (start us, length us, event | category | flops | bytes accessed | tf_op | source)
XLA Modules:
  0.0 36.7 jit_solution(10942811407881540978)
XLA Ops:
  0.6 32.3 %tracer_restart.1 = (f32[40,16,128]{2,1,0:T(8,128)}, f32[2,12,40,128]{3,2,1,0:T(8,128)}, f32[2,12,40,128]{3,2,1,0:T(8,128)}) custom-call(f32[40,16,128]{2,1,0:T(8,128)} %tracer.1, f32[40,16,128]{2,1,0:T(8,128)} %anchor.1, f32[40,16,128]{2,1,0:T(8,128)} %eflow.1, f32[40,16,128]{2,1,0:T(8,128)} %nflow.1, f32[40,16,128]{2,1,0:T(8,128)} %diff.1, ...), custom_call_target="tpu_custom_call" | custom-call | tf_op jit(solution)/shard_map/tracer_restart/pallas_call | solution.py:374
  33.0 0.0 copy-start.1
  33.0 1.8 %copy.13 = f32[40,16,128]{2,1,0:T(8,128)} copy(f32[40,16,128]{2,1,0:T(8,128)} %get-tuple-element.6) | data formatting | bytes 655360
  34.8 0.0 copy-done.1
  34.8 0.0 copy-start
  34.8 0.8 %copy.14 = f32[2,12,40,128]{3,2,1,0:T(8,128)} copy(f32[2,12,40,128]{3,2,1,0:T(8,128)S(1)} %copy-done.1) | data formatting | bytes 983040
  35.5 0.4 %copy-done = f32[2,12,40,128]{3,2,1,0:T(8,128)S(1)} copy-done((f32[2,12,40,128]{3,2,1,0:T(8,128)S(1)}, f32[2,12,40,128]{3,2,1,0:T(8,128)}, u32[]{:S(2)}) %copy-start) | copy-done | bytes 491544
  36.0 0.8 %copy.15 = f32[2,12,40,128]{3,2,1,0:T(8,128)} copy(f32[2,12,40,128]{3,2,1,0:T(8,128)S(1)} %copy-done) | data formatting | bytes 983040
Async XLA Ops:
  33.0 1.8 %copy-start.1 = (f32[2,12,40,128]{3,2,1,0:T(8,128)S(1)}, f32[2,12,40,128]{3,2,1,0:T(8,128)}, u32[]{:S(2)}) copy-start(f32[2,12,40,128]{3,2,1,0:T(8,128)} %get-tuple-element.7) | copy-start | bytes 1474564
  34.8 1.2 %copy-start = (f32[2,12,40,128]{3,2,1,0:T(8,128)S(1)}, f32[2,12,40,128]{3,2,1,0:T(8,128)}, u32[]{:S(2)}) copy-start(f32[2,12,40,128]{3,2,1,0:T(8,128)} %get-tuple-element.8) | copy-start | bytes 1474564
